TPU v7x, 32 devices: a whole 2x2x4 slice. The times are simulated.
32 devices in a mesh: row: 8 (over z, x), col: 4 (over y, core).
Axes of the slice: x: 2, y: 2, z: 4, core: 2. Of those that a mesh axis runs over, the one named last changes fastest.
Arguments:
- panel: float32 [8, 16384, 4, 1024], P('row', None, 'col'), may hold values from -1 to 4, as said below
- rhs: float32 [8, 16384, 256], P('row'), may hold values from -6 to 6
Outputs:
- solved: float32 [4, 1024, 256], P('col')
- remainder: float32 [8, 16384, 256], P('row', None, 'col')
Inputs may be any that keep to these rules, and one draw needn't show every extreme that they name: panel is lower triangular in the global indices: entries with column above row are zero, diagonal entries lie between 2 and 4, the others are of size about 1 / sqrt(4096).
All inputs are finite; a program needn't handle non-finite values.
Results may differ from a plain program's by a relative error of at most 0.000084.
Values sent between devices are 32-bit elements; how exact they have to be, the bound alone decides.
A program may use at most 256 MiB of HBM per device.

v0:
```python
import jax
import jax.numpy as jnp
from jax import lax
from jax.sharding import PartitionSpec as P

TB = 512
BASE = 128
CHUNKS = 4
LANES = 128


def dot(left, right, precision=lax.Precision.HIGHEST):
    return jnp.matmul(left, right, precision=precision, preferred_element_type=jnp.float32)


def invert_lower(tile):
    size = tile.shape[0]
    count = size // BASE
    blocks = jnp.stack(
        [tile[i * BASE : (i + 1) * BASE, i * BASE : (i + 1) * BASE] for i in range(count)]
    )
    eye = jnp.eye(BASE, dtype=jnp.float32)
    scale = 1.0 / jnp.sum(blocks * eye, axis=2)
    power = -jnp.tril(blocks * scale[:, :, None], -1)
    inverse = eye + power
    reach = 2
    while reach < BASE:
        power = dot(power, power)
        inverse = inverse + dot(inverse, power)
        reach *= 2
    inverse = inverse * scale[:, None, :]
    parts = [inverse[i] for i in range(count)]
    width = BASE
    while len(parts) > 1:
        merged = []
        for i in range(0, len(parts), 2):
            lo = i * width
            below = tile[lo + width : lo + 2 * width, lo : lo + width]
            corner = -dot(parts[i + 1], dot(below, parts[i]))
            top = jnp.concatenate([parts[i], jnp.zeros_like(corner)], 1)
            merged.append(jnp.concatenate([top, jnp.concatenate([corner, parts[i + 1]], 1)], 0))
        parts = merged
        width *= 2
    return parts[0]


def pack(value, factor):
    rows = value.shape[0] // factor
    return jnp.concatenate([value[i * rows : (i + 1) * rows] for i in range(factor)], 1)


def unpack(value, factor):
    width = value.shape[1] // factor
    return jnp.concatenate([value[:, i * width : (i + 1) * width] for i in range(factor)], 0)


def on_device(panel, rhs):
    col_count = lax.axis_size("col")
    here_row = lax.axis_index("row")
    here_col = lax.axis_index("col")
    local_panel = panel.reshape(panel.shape[1], panel.shape[3])
    right_side = rhs.reshape(rhs.shape[1], rhs.shape[2])
    rows, width = right_side.shape
    tile_cols = local_panel.shape[1] // TB
    steps = tile_cols * col_count
    top = local_panel[:TB]
    diag_col = jnp.minimum(here_row // col_count, tile_cols - 1)
    has_diag = jnp.logical_and(here_row < steps, here_row % col_count == here_col)
    picked = lax.dynamic_slice_in_dim(top, diag_col * TB, TB, 1)
    diag = lax.psum(jnp.where(has_diag, picked, 0.0), "col")
    diag = jnp.where(here_row < steps, diag, jnp.eye(TB, dtype=jnp.float32))
    inverse = invert_lower(diag)
    tile_of = jnp.arange(tile_cols * TB) // TB * col_count + here_col
    coupling = dot(inverse, jnp.where((tile_of < here_row)[None, :], top, 0.0))
    direct = jnp.where(has_diag, dot(inverse, right_side[:TB]), 0.0)
    own = [jnp.zeros((TB, width), jnp.float32) for _ in range(tile_cols)]
    for step in range(steps):
        term = direct
        known = -(-step // col_count)
        if known:
            stacked = own[0] if known == 1 else jnp.concatenate(own[:known], 0)
            term = direct - dot(coupling[:, : known * TB], stacked)
        block = lax.psum(jnp.where(here_row == step, term, 0.0), ("row", "col"))
        place = step // col_count
        own[place] = jnp.where(here_col == step % col_count, block, own[place])
    own_solved = own[0] if tile_cols == 1 else jnp.concatenate(own, 0)
    chips = col_count // 2
    part = width // col_count
    half = width // 2
    factor = max(1, LANES // part)
    chip = here_col // 2
    core = here_col % 2

    def columns(target_core, hop):
        target = lax.rem(chip - 1 - hop + 2 * chips, chips) * 2 + target_core
        return lax.dynamic_slice_in_dim(own_solved, target * part, part, 1)

    order = [columns(1 - core, hop) for hop in range(chips)]
    order += [columns(core, hop) for hop in range(chips)]
    weights = jnp.concatenate(order, 1)
    swap = [(c, c ^ 1) for c in range(col_count)]
    ring = [(c, (c + 2) % col_count) for c in range(col_count)]
    size = rows // CHUNKS
    pieces = []
    for chunk in range(CHUNKS):
        lo = chunk * size
        product = dot(local_panel[lo : lo + size], weights, lax.Precision.HIGH)
        paired = product[:, half:] + lax.ppermute(product[:, :half], "col", swap)
        total = pack(paired[:, :part], factor)
        for hop in range(1, chips):
            total = lax.ppermute(total, "col", ring)
            total = total + pack(paired[:, hop * part : (hop + 1) * part], factor)
        mine = lax.dynamic_slice(right_side, (lo, here_col * part), (size, part))
        pieces.append(mine - unpack(total, factor))
    remainder = jnp.concatenate(pieces, 0)
    return (own_solved[None], remainder[None])


def solution(mesh):
    return jax.shard_map(
        on_device,
        mesh=mesh,
        in_specs=(P("row", None, "col", None), P("row", None, None)),
        out_specs=(P("col", None, None), P("row", None, "col")),
        check_vma=False,
    )
```

profile of v0, /device:TPU:0, one launch (start us, length us, event | category | flops | bytes accessed | tf_op | source)
XLA Modules:
  0.0 1318.2 jit_solution(84741691303237066)
XLA Ops:
  7.2 3.0 slice.195
  10.3 1.3 copy-done.6
  13.4 39.0 %all-reduce.13.cloned.1.call-done = f32[512,512]{1,0:T(8,128)} async-done(((f32[512,512]{1,0:T(8,128)}), f32[512,512]{1,0:T(8,128)}) %all-reduce.13.cloned.1.call-update) | async-done | bytes 1048592 | tf_op jit(solution)/shard_map/psum | solution.py:70
  52.4 1.3 convert_select_fusion
  60.5 2.8 broadcast_select_fusion.1
  63.6 5.2 fusion.24
  68.8 124.2 %all-reduce.15.cloned.1.call-done = f32[512,256]{1,0:T(8,128)} async-done(((f32[512,256]{1,0:T(8,128)}), f32[512,256]{1,0:T(8,128)}) %all-reduce.15.cloned.1.call-update) | async-done | bytes 524304 | tf_op jit(solution)/shard_map/psum | solution.py:83
  193.0 2.8 fusion.25
  195.9 131.1 %all-reduce.17.cloned.1.call-done = f32[512,256]{1,0:T(8,128)} async-done(((f32[512,256]{1,0:T(8,128)}), f32[512,256]{1,0:T(8,128)}) %all-reduce.17.cloned.1.call-update) | async-done | bytes 524304 | tf_op jit(solution)/shard_map/psum | solution.py:83
  328.1 1.8 fusion.26
  330.0 130.8 %all-reduce.19.cloned.1.call-done = f32[512,256]{1,0:T(8,128)} async-done(((f32[512,256]{1,0:T(8,128)}), f32[512,256]{1,0:T(8,128)}) %all-reduce.19.cloned.1.call-update) | async-done | bytes 524304 | tf_op jit(solution)/shard_map/psum | solution.py:83
  460.8 1.8 fusion.27
  462.7 131.9 %all-reduce.21.cloned.1.call-done = f32[512,256]{1,0:T(8,128)} async-done(((f32[512,256]{1,0:T(8,128)}), f32[512,256]{1,0:T(8,128)}) %all-reduce.21.cloned.1.call-update) | async-done | bytes 524304 | tf_op jit(solution)/shard_map/psum | solution.py:83
  594.6 1.1 broadcast_select_fusion.6
  595.8 1.8 fusion.28
  597.7 130.8 %all-reduce.23.cloned.1.call-done = f32[512,256]{1,0:T(8,128)} async-done(((f32[512,256]{1,0:T(8,128)}), f32[512,256]{1,0:T(8,128)}) %all-reduce.23.cloned.1.call-update) | async-done | bytes 524304 | tf_op jit(solution)/shard_map/psum | solution.py:83
  729.5 2.6 fusion.29
  732.2 130.2 %all-reduce.25.cloned.1.call-done = f32[512,256]{1,0:T(8,128)} async-done(((f32[512,256]{1,0:T(8,128)}), f32[512,256]{1,0:T(8,128)}) %all-reduce.25.cloned.1.call-update) | async-done | bytes 524304 | tf_op jit(solution)/shard_map/psum | solution.py:83
  862.4 1.1 broadcast_select_fusion.2
  864.4 2.6 fusion.30
  867.0 11.2 all-reduce.29.cloned.1.call-start
  878.2 44.1 %fusion.95 = (f32[1,4096,1,1024]{3,2,1,0:T(1,128)}, f32[1,4096,1,1024]{3,2,1,0:T(1,128)}, f32[1,4096,1,1024]{3,2,1,0:T(1,128)}, f32[1,4096,1,1024]{3,2,1,0:T(1,128)}) fusion(f32[1,16384,1,1024]{3,2,1,0:T(1,128)} %param.2), kind=kLoop, calls=%fused_computation.173 | loop fusion | bytes 134217728 | tf_op jit(solution)/shard_map/slice | solution.py:107
  922.2 74.2 %all-reduce.27.cloned.1.call-done = f32[512,256]{1,0:T(8,128)} async-done(((f32[512,256]{1,0:T(8,128)}), f32[512,256]{1,0:T(8,128)}) %all-reduce.27.cloned.1.call-update) | async-done | bytes 524304 | tf_op jit(solution)/shard_map/psum | solution.py:83
  998.3 2.6 fusion.31
  1001.0 8.4 constant_dynamic-slice_fusion.3
  1009.4 3.2 copy.8
  1012.5 3.2 copy.9
  1015.7 3.2 copy.10
  1018.9 1.6 copy.11
  1020.4 110.0 %all-reduce.29.cloned.1.call-done = f32[512,256]{1,0:T(8,128)} async-done(((f32[512,256]{1,0:T(8,128)}), f32[512,256]{1,0:T(8,128)}) %all-reduce.29.cloned.1.call-update) | async-done | bytes 524304 | tf_op jit(solution)/shard_map/psum | solution.py:83
  1131.6 19.6 %fusion.12 = f32[4096,256]{0,1:T(8,128)S(1)} fusion(f32[1024,256]{1,0:T(8,128)S(1)} %pad_maximum_fusion.7, f32[1,4096,1,1024]{3,2,1,0:T(1,128)} %get-tuple-element.2), kind=kOutput, calls=%fused_computation.12 | convolution fusion | flops 6442450944 | bytes 22020096 | tf_op jit(solution)/shard_map/dot_general | solution.py:13
  1151.2 1.6 slice.264
  1153.9 14.2 %fusion.15 = f32[4096,256]{0,1:T(8,128)S(1)} fusion(f32[1024,256]{1,0:T(8,128)S(1)} %pad_maximum_fusion.7, f32[1,4096,1,1024]{3,2,1,0:T(1,128)S(1)} %bitcast.106), kind=kOutput, calls=%fused_computation.13 | convolution fusion | flops 6442450944 | bytes 22020096 | tf_op jit(solution)/shard_map/dot_general | solution.py:13
  1168.1 1.5 slice.272
  1169.6 1.6 copy-done.2
  1171.7 19.4 %fusion.18 = f32[4096,256]{0,1:T(8,128)S(1)} fusion(f32[1024,256]{1,0:T(8,128)S(1)} %pad_maximum_fusion.7, f32[1,4096,1,1024]{3,2,1,0:T(1,128)} %get-tuple-element.5), kind=kOutput, calls=%fused_computation.14 | convolution fusion | flops 6442450944 | bytes 22020096 | tf_op jit(solution)/shard_map/dot_general | solution.py:13
  1191.1 1.6 slice.280
  1194.0 14.3 %fusion.21 = f32[4096,256]{0,1:T(8,128)S(1)} fusion(f32[1024,256]{1,0:T(8,128)S(1)} %pad_maximum_fusion.7, f32[1,4096,1,1024]{3,2,1,0:T(1,128)S(1)} %bitcast.104), kind=kOutput, calls=%fused_computation.15 | convolution fusion | flops 6442450944 | bytes 22020096 | tf_op jit(solution)/shard_map/dot_general | solution.py:13
  1210.8 1.8 slice_add_fusion.3
  1213.0 1.5 collective-permute-start.1
  1214.8 1.9 slice_add_fusion.2
  1217.0 1.5 collective-permute-start.3
  1219.5 1.5 collective-permute-start.5
  1222.2 16.8 %collective-permute-done.1 = f32[2048,128]{0,1:T(8,128)S(1)} collective-permute-done((f32[2048,128]{0,1:T(8,128)S(1)}, f32[2048,128]{0,1:T(8,128)S(1)}, u32[]{:S(2)}, u32[]{:S(2)}) %collective-permute-start.1) | collective-permute-done | bytes 1048608 | tf_op jit(solution)/shard_map/ppermute | solution.py:111
  1239.3 22.3 %collective-permute-done.3 = f32[2048,128]{0,1:T(8,128)S(1)} collective-permute-done((f32[2048,128]{0,1:T(8,128)S(1)}, f32[2048,128]{0,1:T(8,128)S(1)}, u32[]{:S(2)}, u32[]{:S(2)}) %collective-permute-start.3) | collective-permute-done | bytes 1048608 | tf_op jit(solution)/shard_map/ppermute | solution.py:111
  1261.7 22.3 %collective-permute-done.5 = f32[2048,128]{0,1:T(8,128)S(1)} collective-permute-done((f32[2048,128]{0,1:T(8,128)S(1)}, f32[2048,128]{0,1:T(8,128)S(1)}, u32[]{:S(2)}, u32[]{:S(2)}) %collective-permute-start.5) | collective-permute-done | bytes 1048608 | tf_op jit(solution)/shard_map/ppermute | solution.py:111
  1284.2 21.6 %collective-permute-done.7 = f32[2048,128]{0,1:T(8,128)S(1)} collective-permute-done((f32[2048,128]{0,1:T(8,128)S(1)}, f32[2048,128]{0,1:T(8,128)S(1)}, u32[]{:S(2)}, u32[]{:S(2)}) %collective-permute-start.7) | collective-permute-done | bytes 1048608 | tf_op jit(solution)/shard_map/ppermute | solution.py:111
  1308.9 2.3 maximum_bitcast_fusion
  (131 shorter events, 27.1 us)
Async XLA Ops:
  7.2 45.2 %all-reduce.13.cloned.1.call-start = ((), (), s32[]{:S(2)}) async-start(), calls=%async_computation | async-start | bytes 2097152 | tf_op jit(solution)/shard_map/psum | solution.py:70
  10.3 1.3 copy-start.6
  13.2 179.8 %all-reduce.15.cloned.1.call-start = ((), (), s32[]{:S(2)}) async-start(), calls=%async_computation.1 | async-start | bytes 1048576 | tf_op jit(solution)/shard_map/psum | solution.py:83
  63.3 263.7 %all-reduce.17.cloned.1.call-start = ((), (), s32[]{:S(2)}) async-start(), calls=%async_computation.2 | async-start | bytes 1048576 | tf_op jit(solution)/shard_map/psum | solution.py:83
  195.9 264.9 %all-reduce.19.cloned.1.call-start = ((), (), s32[]{:S(2)}) async-start(), calls=%async_computation.3 | async-start | bytes 1048576 | tf_op jit(solution)/shard_map/psum | solution.py:83
  328.1 134.5 %copy-start.7 = (f32[512,256]{1,0:T(8,128)}, f32[512,256]{1,0:T(8,128)S(1)}, u32[]{:S(2)}) copy-start(f32[512,256]{1,0:T(8,128)S(1)} %select_select_fusion) | copy-start | bytes 1572868
  329.9 264.7 %all-reduce.21.cloned.1.call-start = ((), (), s32[]{:S(2)}) async-start(), calls=%async_computation.4 | async-start | bytes 1048576 | tf_op jit(solution)/shard_map/psum | solution.py:83
  462.6 265.8 %all-reduce.23.cloned.1.call-start = ((), (), s32[]{:S(2)}) async-start(), calls=%async_computation.5 | async-start | bytes 1048576 | tf_op jit(solution)/shard_map/psum | solution.py:83
  597.6 264.8 %all-reduce.25.cloned.1.call-start = ((), (), s32[]{:S(2)}) async-start(), calls=%async_computation.6 | async-start | bytes 1048576 | tf_op jit(solution)/shard_map/psum | solution.py:83
  732.2 264.2 %all-reduce.27.cloned.1.call-start = ((), (), s32[]{:S(2)}) async-start(), calls=%async_computation.7 | async-start | bytes 1048576 | tf_op jit(solution)/shard_map/psum | solution.py:83
  863.6 0.8 copy-start.10
  867.0 263.4 %all-reduce.29.cloned.1.call-start = ((), (), s32[]{:S(2)}) async-start(), calls=%async_computation.8 | async-start | bytes 1048576 | tf_op jit(solution)/shard_map/psum | solution.py:83
  997.5 0.8 copy-start.8
  1018.9 111.5 %copy-start.9 = (f32[512,256]{1,0:T(8,128)S(1)}, f32[512,256]{1,0:T(8,128)}, u32[]{:S(2)}) copy-start(f32[512,256]{1,0:T(8,128)} %copy-done.8) | copy-start | bytes 1572868
  1130.5 23.4 %slice-start.4 = ((s8[16777216]{0:T(1024)(128)(4,1)}), s8[4194304]{0:T(1024)(128)(4,1)S(1)}, s32[]{:S(2)}) async-start(s8[16777216]{0:T(1024)(128)(4,1)} %bitcast.105), calls=%async_computation.13 | async-start | bytes 8388608
  1131.6 22.3 %slice-start.5 = ((s8[16777216]{0:T(1024)(128)(4,1)}), s8[4194304]{0:T(1024)(128)(4,1)S(1)}, s32[]{:S(2)}) async-start(s8[16777216]{0:T(1024)(128)(4,1)} %bitcast.105), calls=%async_computation.14 | async-start | bytes 8388608
  1131.6 22.3 %slice-start.6 = ((s8[16777216]{0:T(1024)(128)(4,1)}), s8[4194304]{0:T(1024)(128)(4,1)S(1)}, s32[]{:S(2)}) async-start(s8[16777216]{0:T(1024)(128)(4,1)} %bitcast.105), calls=%async_computation.15 | async-start | bytes 8388608
  1131.6 22.3 %slice-start.7 = ((s8[16777216]{0:T(1024)(128)(4,1)}), s8[4194304]{0:T(1024)(128)(4,1)S(1)}, s32[]{:S(2)}) async-start(s8[16777216]{0:T(1024)(128)(4,1)} %bitcast.105), calls=%async_computation.16 | async-start | bytes 8388608
  1151.2 2.7 copy-start.4
  1153.9 56.0 %collective-permute-start = (f32[4096,128]{0,1:T(8,128)}, f32[4096,128]{0,1:T(8,128)}, u32[]{:S(2)}, u32[]{:S(2)}) collective-permute-start(f32[4096,128]{0,1:T(8,128)} %slice.264), channel_id=1, source_target_pairs={{0,1},{1,0},{2,3},{3,2},{4,5},{5,4},{6,7},{7,6},{8,9},{9,8},{10,11... | collective-permute-start | bytes 6291464 | tf_op jit(solution)/shard_map/ppermute | solution.py:108
  1168.1 3.1 copy-start.2
  1168.1 25.8 %slice-start = ((s8[16777216]{0:T(1024)(128)(4,1)}), s8[4194304]{0:T(1024)(128)(4,1)S(1)}, s32[]{:S(2)}) async-start(s8[16777216]{0:T(1024)(128)(4,1)} %bitcast.103), calls=%async_computation.9 | async-start | bytes 8388608
  1171.2 43.3 %collective-permute-start.2 = (f32[4096,128]{0,1:T(8,128)}, f32[4096,128]{0,1:T(8,128)}, u32[]{:S(2)}, u32[]{:S(2)}) collective-permute-start(f32[4096,128]{0,1:T(8,128)} %slice.272), channel_id=1, source_target_pairs={{0,1},{1,0},{2,3},{3,2},{4,5},{5,4},{6,7},{7,6},{8,9},{9,8},{10,11... | collective-permute-start | bytes 6291464 | tf_op jit(solution)/shard_map/ppermute | solution.py:108
  1171.7 22.2 %slice-start.1 = ((s8[16777216]{0:T(1024)(128)(4,1)}), s8[4194304]{0:T(1024)(128)(4,1)S(1)}, s32[]{:S(2)}) async-start(s8[16777216]{0:T(1024)(128)(4,1)} %bitcast.103), calls=%async_computation.10 | async-start | bytes 8388608
  1171.7 22.2 %slice-start.2 = ((s8[16777216]{0:T(1024)(128)(4,1)}), s8[4194304]{0:T(1024)(128)(4,1)S(1)}, s32[]{:S(2)}) async-start(s8[16777216]{0:T(1024)(128)(4,1)} %bitcast.103), calls=%async_computation.11 | async-start | bytes 8388608
  1171.7 22.2 %slice-start.3 = ((s8[16777216]{0:T(1024)(128)(4,1)}), s8[4194304]{0:T(1024)(128)(4,1)S(1)}, s32[]{:S(2)}) async-start(s8[16777216]{0:T(1024)(128)(4,1)} %bitcast.103), calls=%async_computation.12 | async-start | bytes 8388608
  1191.1 2.6 copy-start
  1193.7 24.8 %collective-permute-start.4 = (f32[4096,128]{0,1:T(8,128)}, f32[4096,128]{0,1:T(8,128)S(1)}, u32[]{:S(2)}, u32[]{:S(2)}) collective-permute-start(f32[4096,128]{0,1:T(8,128)} %slice.280), channel_id=1, source_target_pairs={{0,1},{1,0},{2,3},{3,2},{4,5},{5,4},{6,7},{7,6},{8,9},{9,8},{10,11... | collective-permute-start | bytes 6291464 | tf_op jit(solution)/shard_map/ppermute | solution.py:108
  1208.2 2.6 copy-start.5
  1208.4 12.6 collective-permute-start.6
  1212.6 2.2 copy-start.3
  1213.0 26.1 %collective-permute-start.1 = (f32[2048,128]{0,1:T(8,128)S(1)}, f32[2048,128]{0,1:T(8,128)S(1)}, u32[]{:S(2)}, u32[]{:S(2)}) collective-permute-start(f32[2048,128]{0,1:T(8,128)S(1)} %pad_maximum_fusion.8), channel_id=1, source_target_pairs={{0,2},{1,3},{2,0},{3,1},{4,6},{5,7},{6,4},{7,5},{8,10},{9,11},{10,... | collective-permute-start | bytes 3145736 | tf_op jit(solution)/shard_map/ppermute | solution.py:111
  1216.7 2.2 copy-start.1
  1217.0 44.5 %collective-permute-start.3 = (f32[2048,128]{0,1:T(8,128)S(1)}, f32[2048,128]{0,1:T(8,128)S(1)}, u32[]{:S(2)}, u32[]{:S(2)}) collective-permute-start(f32[2048,128]{0,1:T(8,128)S(1)} %pad_maximum_fusion.9), channel_id=1, source_target_pairs={{0,2},{1,3},{2,0},{3,1},{4,6},{5,7},{6,4},{7,5},{8,10},{9,11},{10,... | collective-permute-start | bytes 3145736 | tf_op jit(solution)/shard_map/ppermute | solution.py:111
  1219.5 64.5 %collective-permute-start.5 = (f32[2048,128]{0,1:T(8,128)S(1)}, f32[2048,128]{0,1:T(8,128)S(1)}, u32[]{:S(2)}, u32[]{:S(2)}) collective-permute-start(f32[2048,128]{0,1:T(8,128)S(1)} %pad_maximum_fusion.10), channel_id=1, source_target_pairs={{0,2},{1,3},{2,0},{3,1},{4,6},{5,7},{6,4},{7,5},{8,10},{9,11},{10,... | collective-permute-start | bytes 3145736 | tf_op jit(solution)/shard_map/ppermute | solution.py:111
  1221.6 84.2 %collective-permute-start.7 = (f32[2048,128]{0,1:T(8,128)S(1)}, f32[2048,128]{0,1:T(8,128)S(1)}, u32[]{:S(2)}, u32[]{:S(2)}) collective-permute-start(f32[2048,128]{0,1:T(8,128)S(1)} %pad_maximum_fusion.11), channel_id=1, source_target_pairs={{0,2},{1,3},{2,0},{3,1},{4,6},{5,7},{6,4},{7,5},{8,10},{9,11},{10,... | collective-permute-start | bytes 3145736 | tf_op jit(solution)/shard_map/ppermute | solution.py:111
  1305.8 1.2 copy-start.14
  1306.1 1.3 copy-start.13
  1307.1 1.3 copy-start.12
  1307.5 1.3 copy-start.11
Sparse Core Ops, SparseCore 0:
  13.3 38.9 all-reduce.12
  63.4 129.5 all-reduce.14
  198.9 128.0 all-reduce.16
  332.7 128.0 all-reduce.18
  466.5 128.0 all-reduce.20
  600.3 128.0 all-reduce.22
  734.3 128.0 all-reduce.24
  868.3 128.0 all-reduce.26
  1002.3 128.0 all-reduce.28
where the time goes:
time: 1330 us; the launch traced here: 1320 us
  waiting for transfers between devices  1090 us (82%)
  matrix products  97.8 us (7%)
  local copies, waits for them, and re-layouts  83.9 us (6%)
  other arithmetic  18.2 us (1%)
  starting transfers between devices  18 us (1%)
  between operations  15.1 us (1%)
    psum x8, waiting for transfers between devices, on_device(): block = lax.psum(jnp.where(here_row == step, term, 0.0), ('row', 'col'))  963 us
    dot_general x31, matrix products, dot(): jnp.matmul(left, right, precision=precision, preferred_element_type=jnp.f...  97.8 us
    ppermute x4, waiting for transfers between devices, on_device(): total = lax.ppermute(total, 'col', ring)  82.9 us
    slice x1, local copies, waits for them, and re-layouts, on_device(): product = dot(local_panel[lo:lo + size], weights, lax.Precision.HIGH)  44.1 us
    psum x1, waiting for transfers between devices, on_device(): diag = lax.psum(jnp.where(has_diag, picked, 0.0), 'col')  39 us
  transfers between devices with their start and end apart: 17, of which 13 were waited for; matrix products, arithmetic and copies ran while one was open for 10% of the time, Pallas kernels for 0%

commit v1 on v0

--- a/solution.py
+++ b/solution.py
@@ -80,7 +80,9 @@
         if known:
             stacked = own[0] if known == 1 else jnp.concatenate(own[:known], 0)
             term = direct - dot(coupling[:, : known * TB], stacked)
-        block = lax.psum(jnp.where(here_row == step, term, 0.0), ("row", "col"))
+        block = jnp.sum(
+            lax.all_gather(jnp.where(here_row == step, term, 0.0), ("row", "col")), axis=0
+        )
         place = step // col_count
         own[place] = jnp.where(here_col == step % col_count, block, own[place])
     own_solved = own[0] if tile_cols == 1 else jnp.concatenate(own, 0)

time: 1330 us -> 1250 us (0.940)
  waiting for transfers between devices: 1090 us -> 954 us
  other arithmetic: 18.2 us -> 79.7 us
    psum x8 -> x0, waiting for transfers between devices: 963 us -> none  [on_device(): block = lax.psum(jnp.where(here_row == step, term, 0.0), ('row', 'col'))]
    all_gather x0 -> x8, waiting for transfers between devices: none -> 833 us  [on_device(): lax.all_gather(jnp.where(here_row == step, term, 0.0), ('row', 'col'))]
    reduce_sum x0 -> x8, other arithmetic: none -> 59.9 us  [on_device(): jnp.sum(lax.all_gather(jnp.where(here_row == step, term, 0.0), ('row', 'c...]
where the time goes in v1:
time: 1250 us; the launch traced here: 1240 us
  waiting for transfers between devices  954 us (76%)
  matrix products  96.7 us (8%)
  local copies, waits for them, and re-layouts  84.8 us (7%)
  other arithmetic  79.7 us (6%)
  between operations  14.9 us (1%)
    all_gather x8, waiting for transfers between devices, on_device(): lax.all_gather(jnp.where(here_row == step, term, 0.0), ('row', 'col'))  833 us
    dot_general x31, matrix products, dot(): jnp.matmul(left, right, precision=precision, preferred_element_type=jnp.f...  96.7 us
    ppermute x4, waiting for transfers between devices, on_device(): total = lax.ppermute(total, 'col', ring)  81.3 us
    reduce_sum x8, other arithmetic, on_device(): jnp.sum(lax.all_gather(jnp.where(here_row == step, term, 0.0), ('row', 'c...  59.9 us
    slice x1, local copies, waits for them, and re-layouts, on_device(): product = dot(local_panel[lo:lo + size], weights, lax.Precision.HIGH)  45.1 us
    psum x1, waiting for transfers between devices, on_device(): diag = lax.psum(jnp.where(has_diag, picked, 0.0), 'col')  39 us
  transfers between devices with their start and end apart: 17, of which 13 were waited for; matrix products, arithmetic and copies ran while one was open for 10% of the time, Pallas kernels for 0%

profile of v1, /device:TPU:0, one launch (start us, length us, event | category | flops | bytes accessed | tf_op | source)
XLA Modules:
  0.0 1237.5 jit_solution(14048239833273487301)
XLA Ops:
  7.2 3.0 slice.195
  13.4 39.0 %all-reduce.5.cloned.1.call-done = f32[512,512]{1,0:T(8,128)} async-done(((f32[512,512]{1,0:T(8,128)}), f32[512,512]{1,0:T(8,128)}) %all-reduce.5.cloned.1.call-update) | async-done | bytes 1048592 | tf_op jit(solution)/shard_map/psum | solution.py:70
  60.5 2.8 broadcast_select_fusion.1
  63.6 5.2 fusion.24
  68.8 109.5 %all-gather.17.cloned.1.call-done = f32[16384,256]{1,0:T(8,128)} async-done(((f32[512,256]{1,0:T(8,128)}), f32[16384,256]{1,0:T(8,128)}) %all-gather.17.cloned.1.call-update) | async-done | bytes 16777232 | tf_op jit(solution)/shard_map/all_gather | solution.py:84
  178.3 6.9 reduce_sum.82
  185.2 1.8 fusion.25
  187.1 112.7 %all-gather.19.cloned.1.call-done = f32[16384,256]{1,0:T(8,128)} async-done(((f32[512,256]{1,0:T(8,128)}), f32[16384,256]{1,0:T(8,128)}) %all-gather.19.cloned.1.call-update) | async-done | bytes 16777232 | tf_op jit(solution)/shard_map/all_gather | solution.py:84
  299.7 7.7 reduce_sum.83
  308.5 1.8 fusion.26
  310.4 112.4 %all-gather.21.cloned.1.call-done = f32[16384,256]{1,0:T(8,128)} async-done(((f32[512,256]{1,0:T(8,128)}), f32[16384,256]{1,0:T(8,128)}) %all-gather.21.cloned.1.call-update) | async-done | bytes 16777232 | tf_op jit(solution)/shard_map/all_gather | solution.py:84
  422.8 7.7 reduce_sum.84
  430.5 1.8 fusion.27
  432.6 113.5 %all-gather.23.cloned.1.call-done = f32[16384,256]{1,0:T(8,128)} async-done(((f32[512,256]{1,0:T(8,128)}), f32[16384,256]{1,0:T(8,128)}) %all-gather.23.cloned.1.call-update) | async-done | bytes 16777232 | tf_op jit(solution)/shard_map/all_gather | solution.py:84
  546.1 7.7 reduce_sum.85
  554.9 1.8 fusion.28
  556.8 112.7 %all-gather.25.cloned.1.call-done = f32[16384,256]{1,0:T(8,128)} async-done(((f32[512,256]{1,0:T(8,128)}), f32[16384,256]{1,0:T(8,128)}) %all-gather.25.cloned.1.call-update) | async-done | bytes 16777232 | tf_op jit(solution)/shard_map/all_gather | solution.py:84
  669.5 7.7 reduce_sum.86
  678.2 2.6 fusion.29
  680.9 112.4 %all-gather.27.cloned.1.call-done = f32[16384,256]{1,0:T(8,128)} async-done(((f32[512,256]{1,0:T(8,128)}), f32[16384,256]{1,0:T(8,128)}) %all-gather.27.cloned.1.call-update) | async-done | bytes 16777232 | tf_op jit(solution)/shard_map/all_gather | solution.py:84
  793.4 7.7 reduce_sum.87
  802.9 2.6 fusion.30
  806.0 112.0 %all-gather.29.cloned.1.call-done = f32[16384,256]{1,0:T(8,128)} async-done(((f32[512,256]{1,0:T(8,128)}), f32[16384,256]{1,0:T(8,128)}) %all-gather.29.cloned.1.call-update) | async-done | bytes 16777232 | tf_op jit(solution)/shard_map/all_gather | solution.py:84
  918.1 7.7 reduce_sum.88
  927.6 2.6 fusion.31
  930.3 8.4 constant_dynamic-slice_fusion.3
  938.7 3.2 copy.8
  941.9 3.2 copy.9
  945.1 3.2 copy.10
  948.2 1.6 copy.11
  949.8 45.1 %fusion.95 = (f32[1,4096,1,1024]{3,2,1,0:T(1,128)}, f32[1,4096,1,1024]{3,2,1,0:T(1,128)}, f32[1,4096,1,1024]{3,2,1,0:T(1,128)}, f32[1,4096,1,1024]{3,2,1,0:T(1,128)}) fusion(f32[1,16384,1,1024]{3,2,1,0:T(1,128)} %param.2), kind=kLoop, calls=%fused_computation.173 | loop fusion | bytes 134217728 | tf_op jit(solution)/shard_map/slice | solution.py:109
  994.9 48.1 %all-gather.31.cloned.1.call-done = f32[16384,256]{1,0:T(8,128)} async-done(((f32[512,256]{1,0:T(8,128)}), f32[16384,256]{1,0:T(8,128)}) %all-gather.31.cloned.1.call-update) | async-done | bytes 16777232 | tf_op jit(solution)/shard_map/all_gather | solution.py:84
  1043.0 6.9 reduce_sum.89
  1051.2 19.4 %fusion.12 = f32[4096,256]{0,1:T(8,128)S(1)} fusion(f32[1024,256]{1,0:T(8,128)S(1)} %pad_maximum_fusion.7, f32[1,4096,1,1024]{3,2,1,0:T(1,128)} %get-tuple-element.2), kind=kOutput, calls=%fused_computation.12 | convolution fusion | flops 6442450944 | bytes 22020096 | tf_op jit(solution)/shard_map/dot_general | solution.py:13
  1070.6 1.6 slice.264
  1073.4 14.4 %fusion.15 = f32[4096,256]{0,1:T(8,128)S(1)} fusion(f32[1024,256]{1,0:T(8,128)S(1)} %pad_maximum_fusion.7, f32[1,4096,1,1024]{3,2,1,0:T(1,128)S(1)} %bitcast.114), kind=kOutput, calls=%fused_computation.13 | convolution fusion | flops 6442450944 | bytes 22020096 | tf_op jit(solution)/shard_map/dot_general | solution.py:13
  1089.4 1.7 copy-done.2
  1091.3 19.3 %fusion.18 = f32[4096,256]{0,1:T(8,128)S(1)} fusion(f32[1024,256]{1,0:T(8,128)S(1)} %pad_maximum_fusion.7, f32[1,4096,1,1024]{3,2,1,0:T(1,128)} %get-tuple-element.5), kind=kOutput, calls=%fused_computation.14 | convolution fusion | flops 6442450944 | bytes 22020096 | tf_op jit(solution)/shard_map/dot_general | solution.py:13
  1110.6 1.6 slice.280
  1113.5 14.2 %fusion.21 = f32[4096,256]{0,1:T(8,128)S(1)} fusion(f32[1024,256]{1,0:T(8,128)S(1)} %pad_maximum_fusion.7, f32[1,4096,1,1024]{3,2,1,0:T(1,128)S(1)} %bitcast.112), kind=kOutput, calls=%fused_computation.15 | convolution fusion | flops 6442450944 | bytes 22020096 | tf_op jit(solution)/shard_map/dot_general | solution.py:13
  1130.3 1.9 slice_add_fusion.3
  1134.4 1.9 slice_add_fusion.2
  1138.4 1.9 slice_add_fusion.1
  1143.4 15.2 %collective-permute-done.1 = f32[2048,128]{0,1:T(8,128)S(1)} collective-permute-done((f32[2048,128]{0,1:T(8,128)S(1)}, f32[2048,128]{0,1:T(8,128)S(1)}, u32[]{:S(2)}, u32[]{:S(2)}) %collective-permute-start.1) | collective-permute-done | bytes 1048608 | tf_op jit(solution)/shard_map/ppermute | solution.py:113
  1158.8 22.3 %collective-permute-done.3 = f32[2048,128]{0,1:T(8,128)S(1)} collective-permute-done((f32[2048,128]{0,1:T(8,128)S(1)}, f32[2048,128]{0,1:T(8,128)S(1)}, u32[]{:S(2)}, u32[]{:S(2)}) %collective-permute-start.3) | collective-permute-done | bytes 1048608 | tf_op jit(solution)/shard_map/ppermute | solution.py:113
  1181.3 22.3 %collective-permute-done.5 = f32[2048,128]{0,1:T(8,128)S(1)} collective-permute-done((f32[2048,128]{0,1:T(8,128)S(1)}, f32[2048,128]{0,1:T(8,128)S(1)}, u32[]{:S(2)}, u32[]{:S(2)}) %collective-permute-start.5) | collective-permute-done | bytes 1048608 | tf_op jit(solution)/shard_map/ppermute | solution.py:113
  1203.8 21.5 %collective-permute-done.7 = f32[2048,128]{0,1:T(8,128)S(1)} collective-permute-done((f32[2048,128]{0,1:T(8,128)S(1)}, f32[2048,128]{0,1:T(8,128)S(1)}, u32[]{:S(2)}, u32[]{:S(2)}) %collective-permute-start.7) | collective-permute-done | bytes 1048608 | tf_op jit(solution)/shard_map/ppermute | solution.py:113
  1228.4 2.3 maximum_bitcast_fusion
  (141 shorter events, 38.4 us)
Async XLA Ops:
  7.2 45.2 %all-reduce.5.cloned.1.call-start = ((), (), s32[]{:S(2)}) async-start(), calls=%async_computation | async-start | bytes 2097152 | tf_op jit(solution)/shard_map/psum | solution.py:70
  10.3 1.3 copy-start.6
  13.2 165.1 %all-gather.17.cloned.1.call-start = ((), (), s32[]{:S(2)}) async-start(), calls=%async_computation.1 | async-start | bytes 17301504 | tf_op jit(solution)/shard_map/all_gather | solution.py:84
  63.3 236.4 %all-gather.19.cloned.1.call-start = ((), (), s32[]{:S(2)}) async-start(), calls=%async_computation.2 | async-start | bytes 17301504 | tf_op jit(solution)/shard_map/all_gather | solution.py:84
  185.2 114.5 %copy-start.10 = (f32[512,256]{1,0:T(8,128)}, f32[512,256]{1,0:T(8,128)S(1)}, u32[]{:S(2)}) copy-start(f32[512,256]{1,0:T(8,128)S(1)} %reduce_sum.82) | copy-start | bytes 1572868
  187.0 235.8 %all-gather.21.cloned.1.call-start = ((), (), s32[]{:S(2)}) async-start(), calls=%async_computation.3 | async-start | bytes 17301504 | tf_op jit(solution)/shard_map/all_gather | solution.py:84
  308.5 122.0 %copy-start.7 = (f32[512,256]{1,0:T(8,128)}, f32[512,256]{1,0:T(8,128)S(1)}, u32[]{:S(2)}) copy-start(f32[512,256]{1,0:T(8,128)S(1)} %select_select_fusion) | copy-start | bytes 1572868
  310.3 235.7 %all-gather.23.cloned.1.call-start = ((), (), s32[]{:S(2)}) async-start(), calls=%async_computation.4 | async-start | bytes 17301504 | tf_op jit(solution)/shard_map/all_gather | solution.py:84
  432.3 237.2 %all-gather.25.cloned.1.call-start = ((), (), s32[]{:S(2)}) async-start(), calls=%async_computation.5 | async-start | bytes 17301504 | tf_op jit(solution)/shard_map/all_gather | solution.py:84
  556.7 236.6 %all-gather.27.cloned.1.call-start = ((), (), s32[]{:S(2)}) async-start(), calls=%async_computation.6 | async-start | bytes 17301504 | tf_op jit(solution)/shard_map/all_gather | solution.py:84
  680.9 237.2 %all-gather.29.cloned.1.call-start = ((), (), s32[]{:S(2)}) async-start(), calls=%async_computation.7 | async-start | bytes 17301504 | tf_op jit(solution)/shard_map/all_gather | solution.py:84
  802.1 0.8 copy-start.11
  805.6 237.4 %all-gather.31.cloned.1.call-start = ((), (), s32[]{:S(2)}) async-start(), calls=%async_computation.8 | async-start | bytes 17301504 | tf_op jit(solution)/shard_map/all_gather | solution.py:84
  926.9 0.8 copy-start.8
  1043.0 6.9 copy-start.9
  1050.0 23.4 %slice-start.4 = ((s8[16777216]{0:T(1024)(128)(4,1)}), s8[4194304]{0:T(1024)(128)(4,1)S(1)}, s32[]{:S(2)}) async-start(s8[16777216]{0:T(1024)(128)(4,1)} %bitcast.113), calls=%async_computation.13 | async-start | bytes 8388608
  1051.1 22.3 %slice-start.5 = ((s8[16777216]{0:T(1024)(128)(4,1)}), s8[4194304]{0:T(1024)(128)(4,1)S(1)}, s32[]{:S(2)}) async-start(s8[16777216]{0:T(1024)(128)(4,1)} %bitcast.113), calls=%async_computation.14 | async-start | bytes 8388608
  1051.1 22.3 %slice-start.6 = ((s8[16777216]{0:T(1024)(128)(4,1)}), s8[4194304]{0:T(1024)(128)(4,1)S(1)}, s32[]{:S(2)}) async-start(s8[16777216]{0:T(1024)(128)(4,1)} %bitcast.113), calls=%async_computation.15 | async-start | bytes 8388608
  1051.2 22.3 %slice-start.7 = ((s8[16777216]{0:T(1024)(128)(4,1)}), s8[4194304]{0:T(1024)(128)(4,1)S(1)}, s32[]{:S(2)}) async-start(s8[16777216]{0:T(1024)(128)(4,1)} %bitcast.113), calls=%async_computation.16 | async-start | bytes 8388608
  1070.6 2.6 copy-start.4
  1073.2 56.1 %collective-permute-start = (f32[4096,128]{0,1:T(8,128)}, f32[4096,128]{0,1:T(8,128)}, u32[]{:S(2)}, u32[]{:S(2)}) collective-permute-start(f32[4096,128]{0,1:T(8,128)} %slice.264), channel_id=1, source_target_pairs={{0,1},{1,0},{2,3},{3,2},{4,5},{5,4},{6,7},{7,6},{8,9},{9,8},{10,11... | collective-permute-start | bytes 6291464 | tf_op jit(solution)/shard_map/ppermute | solution.py:110
  1087.9 3.1 copy-start.2
  1087.9 25.6 %slice-start = ((s8[16777216]{0:T(1024)(128)(4,1)}), s8[4194304]{0:T(1024)(128)(4,1)S(1)}, s32[]{:S(2)}) async-start(s8[16777216]{0:T(1024)(128)(4,1)} %bitcast.111), calls=%async_computation.9 | async-start | bytes 8388608
  1091.0 43.0 %collective-permute-start.2 = (f32[4096,128]{0,1:T(8,128)}, f32[4096,128]{0,1:T(8,128)}, u32[]{:S(2)}, u32[]{:S(2)}) collective-permute-start(f32[4096,128]{0,1:T(8,128)} %slice.272), channel_id=1, source_target_pairs={{0,1},{1,0},{2,3},{3,2},{4,5},{5,4},{6,7},{7,6},{8,9},{9,8},{10,11... | collective-permute-start | bytes 6291464 | tf_op jit(solution)/shard_map/ppermute | solution.py:110
  1091.3 22.2 %slice-start.1 = ((s8[16777216]{0:T(1024)(128)(4,1)}), s8[4194304]{0:T(1024)(128)(4,1)S(1)}, s32[]{:S(2)}) async-start(s8[16777216]{0:T(1024)(128)(4,1)} %bitcast.111), calls=%async_computation.10 | async-start | bytes 8388608
  1091.3 22.2 %slice-start.2 = ((s8[16777216]{0:T(1024)(128)(4,1)}), s8[4194304]{0:T(1024)(128)(4,1)S(1)}, s32[]{:S(2)}) async-start(s8[16777216]{0:T(1024)(128)(4,1)} %bitcast.111), calls=%async_computation.11 | async-start | bytes 8388608
  1091.3 22.2 %slice-start.3 = ((s8[16777216]{0:T(1024)(128)(4,1)}), s8[4194304]{0:T(1024)(128)(4,1)S(1)}, s32[]{:S(2)}) async-start(s8[16777216]{0:T(1024)(128)(4,1)} %bitcast.111), calls=%async_computation.12 | async-start | bytes 8388608
  1110.6 2.6 copy-start
  1113.2 24.9 %collective-permute-start.4 = (f32[4096,128]{0,1:T(8,128)}, f32[4096,128]{0,1:T(8,128)}, u32[]{:S(2)}, u32[]{:S(2)}) collective-permute-start(f32[4096,128]{0,1:T(8,128)} %slice.280), channel_id=1, source_target_pairs={{0,1},{1,0},{2,3},{3,2},{4,5},{5,4},{6,7},{7,6},{8,9},{9,8},{10,11... | collective-permute-start | bytes 6291464 | tf_op jit(solution)/shard_map/ppermute | solution.py:110
  1127.8 2.6 copy-start.5
  1127.9 14.2 %collective-permute-start.6 = (f32[4096,128]{0,1:T(8,128)S(1)}, f32[4096,128]{0,1:T(8,128)S(1)}, u32[]{:S(2)}, u32[]{:S(2)}) collective-permute-start(f32[4096,128]{0,1:T(8,128)S(1)} %slice.288), channel_id=1, source_target_pairs={{0,1},{1,0},{2,3},{3,2},{4,5},{5,4},{6,7},{7,6},{8,9},{9,8},{10,11... | collective-permute-start | bytes 6291464 | tf_op jit(solution)/shard_map/ppermute | solution.py:110
  1132.2 2.2 copy-start.3
  1132.5 26.1 %collective-permute-start.1 = (f32[2048,128]{0,1:T(8,128)S(1)}, f32[2048,128]{0,1:T(8,128)S(1)}, u32[]{:S(2)}, u32[]{:S(2)}) collective-permute-start(f32[2048,128]{0,1:T(8,128)S(1)} %pad_maximum_fusion.8), channel_id=1, source_target_pairs={{0,2},{1,3},{2,0},{3,1},{4,6},{5,7},{6,4},{7,5},{8,10},{9,11},{10,... | collective-permute-start | bytes 3145736 | tf_op jit(solution)/shard_map/ppermute | solution.py:113
  1136.2 2.2 copy-start.1
  1136.6 44.5 %collective-permute-start.3 = (f32[2048,128]{0,1:T(8,128)S(1)}, f32[2048,128]{0,1:T(8,128)S(1)}, u32[]{:S(2)}, u32[]{:S(2)}) collective-permute-start(f32[2048,128]{0,1:T(8,128)S(1)} %pad_maximum_fusion.9), channel_id=1, source_target_pairs={{0,2},{1,3},{2,0},{3,1},{4,6},{5,7},{6,4},{7,5},{8,10},{9,11},{10,... | collective-permute-start | bytes 3145736 | tf_op jit(solution)/shard_map/ppermute | solution.py:113
  1140.6 62.9 %collective-permute-start.5 = (f32[2048,128]{0,1:T(8,128)S(1)}, f32[2048,128]{0,1:T(8,128)S(1)}, u32[]{:S(2)}, u32[]{:S(2)}) collective-permute-start(f32[2048,128]{0,1:T(8,128)S(1)} %pad_maximum_fusion.10), channel_id=1, source_target_pairs={{0,2},{1,3},{2,0},{3,1},{4,6},{5,7},{6,4},{7,5},{8,10},{9,11},{10,... | collective-permute-start | bytes 3145736 | tf_op jit(solution)/shard_map/ppermute | solution.py:113
  1142.7 82.6 %collective-permute-start.7 = (f32[2048,128]{0,1:T(8,128)S(1)}, f32[2048,128]{0,1:T(8,128)S(1)}, u32[]{:S(2)}, u32[]{:S(2)}) collective-permute-start(f32[2048,128]{0,1:T(8,128)S(1)} %pad_maximum_fusion.11), channel_id=1, source_target_pairs={{0,2},{1,3},{2,0},{3,1},{4,6},{5,7},{6,4},{7,5},{8,10},{9,11},{10,... | collective-permute-start | bytes 3145736 | tf_op jit(solution)/shard_map/ppermute | solution.py:113
  1225.3 1.2 copy-start.15
  1225.6 1.3 copy-start.14
  1226.6 1.3 copy-start.13
  1227.0 1.3 copy-start.12
Sparse Core Ops, SparseCore 0:
  13.3 38.9 all-reduce.4
  63.4 114.7 all-gather.16
  187.1 112.5 all-gather.18
  310.4 112.3 all-gather.20
  432.4 113.5 all-gather.22
  556.8 112.5 all-gather.24
  681.0 112.3 all-gather.26
  805.7 112.3 all-gather.28
  930.4 112.5 all-gather.30
